TPU v7x, 256 devices: a whole 4x4x8 slice. The times are simulated.
256 devices in a mesh: gx: 16 (over z_lo, x), gy: 4 (over z_hi, core), gz: 4 (over y).
Axes of the slice: x: 4, y: 4, z: 8 (z_hi: 2, z_lo: 4; z = z_hi * 4 + z_lo), core: 2. Of those that a mesh axis runs over, the one named last changes fastest.
Arguments:
- inverse_blocks: bfloat16 [50, 50, 98304], P(None, None, ('gx', 'gy', 'gz')), may hold values from -0.875 to 0.875
- face_blocks: bfloat16 [4, 50, 50, 98304], P(None, None, None, ('gx', 'gy', 'gz')), may hold values from -0.4375 to 0.4375
- load_vector: bfloat16 [50, 8, 98304], P(None, None, ('gx', 'gy', 'gz')), may hold values from -6 to 6
- live_counts: int32 [256], P(('gx', 'gy', 'gz')), may hold values from 192 to 384, as said below
- nbr_kind: int32 [4, 98304], P(None, ('gx', 'gy', 'gz')), may hold values from 0 to 7, as said below
- nbr_slot: int32 [4, 98304], P(None, ('gx', 'gy', 'gz')), may hold values from 0 to 383, as said below
- send_x: int32 [256, 2, 128], P(('gx', 'gy', 'gz')), may hold values from 0 to 383, as said below
- send_yz: int32 [256, 4, 64], P(('gx', 'gy', 'gz')), may hold values from 0 to 383, as said below
Outputs:
- adjoint: bfloat16 [50, 8, 98304], P(None, None, ('gx', 'gy', 'gz'))
Inputs may be any that keep to these rules, and one draw needn't show every extreme that they name: Device d has live_counts[d] live elements, at least 192; some device has 384. `nbr_kind`: 0 means no neighbour, 1 a neighbour on the same device, 2 + j a neighbour received from direction j; a direction whose source device does not exist is never named; faces of slots that are not live are 0. `nbr_slot`: for kind 1 a live element of the same device; for kinds 2 and 3 below 128; for kinds 4 to 7 below 64; 0 for kind 0. `send_x`: live elements of the sending device; the entries of one device's list for one direction are distinct. `send_yz`: live elements of the sending device; the entries of one device's list for one direction are distinct.
All inputs are finite; a program needn't handle non-finite values.
Results may differ from a plain program's by a relative error of at most 0.012.
Values may be sent and summed in bfloat16 or wider, within the bound.
A program may use at most 128 MiB of HBM per device.

v0:
```python
import jax
import jax.numpy as jnp
from jax import lax
from jax.sharding import PartitionSpec as P

SWEEPS = 2


def passed_along(shard, axis, by):
    length = lax.axis_size(axis)
    pairs = [(i, i + by) for i in range(length) if 0 <= i + by < length]
    return lax.ppermute(shard, axis, pairs)


def block_apply(blocks, vectors):
    product = blocks[:, :, None, :].astype(jnp.float32) * vectors[None, :, :, :].astype(jnp.float32)
    return jnp.sum(product, axis=1)


def exchange_faces(adjoint, list_x, list_yz):
    outgoing = [jnp.take(adjoint, list_x[0], axis=2), jnp.take(adjoint, list_x[1], axis=2)]
    for direction in range(4):
        outgoing.append(jnp.take(adjoint, list_yz[direction], axis=2))
    return [
        passed_along(outgoing[0], "gx", 1),
        passed_along(outgoing[1], "gx", -1),
        passed_along(outgoing[2], "gy", 1),
        passed_along(outgoing[3], "gy", -1),
        passed_along(outgoing[4], "gz", 1),
        passed_along(outgoing[5], "gz", -1),
    ]


def shards(
    inverse_blocks, face_blocks, load_vector, live_counts, nbr_kind, nbr_slot, send_x, send_yz
):
    unknowns = load_vector.shape[0]
    targets = load_vector.shape[1]
    elements = load_vector.shape[2]
    faces = nbr_kind.shape[0]
    width_x = send_x.shape[2]
    width_yz = send_yz.shape[2]
    live_mask = jnp.arange(elements, dtype=jnp.int32) < live_counts[0]
    offset_list = [elements, elements + width_x]
    for direction in range(4):
        offset_list.append(elements + 2 * width_x + direction * width_yz)
    lookup = jnp.where(nbr_kind == 1, nbr_slot, 0)
    for direction in range(6):
        lookup = jnp.where(nbr_kind == direction + 2, offset_list[direction] + nbr_slot, lookup)
    flat_lookup = lookup.reshape(faces * elements)
    active = nbr_kind > 0
    adjoint = jnp.where(live_mask, block_apply(inverse_blocks, load_vector), 0.0).astype(
        jnp.bfloat16
    )
    load_wide = load_vector.astype(jnp.float32)
    for repeat in range(SWEEPS):
        received = exchange_faces(adjoint, send_x[0], send_yz[0])
        gathered = jnp.concatenate([adjoint] + received, axis=2)
        picked = jnp.take(gathered, flat_lookup, axis=2).reshape(unknowns, targets, faces, elements)
        coupling = jnp.zeros(load_vector.shape, jnp.float32)
        for face in range(faces):
            beside = jnp.where(active[face], picked[:, :, face, :], jnp.zeros((), jnp.bfloat16))
            coupling = coupling + block_apply(face_blocks[face], beside)
        residual = (load_wide - coupling).astype(jnp.bfloat16)
        adjoint = jnp.where(live_mask, block_apply(inverse_blocks, residual), 0.0).astype(
            jnp.bfloat16
        )
    return adjoint


def solution(mesh):
    placed = (
        P(None, None, ("gx", "gy", "gz")),
        P(None, None, None, ("gx", "gy", "gz")),
        P(None, None, ("gx", "gy", "gz")),
        P(("gx", "gy", "gz")),
        P(None, ("gx", "gy", "gz")),
        P(None, ("gx", "gy", "gz")),
        P(("gx", "gy", "gz"), None, None),
        P(("gx", "gy", "gz"), None, None),
    )
    return jax.shard_map(
        shards,
        mesh=mesh,
        in_specs=placed,
        out_specs=P(None, None, ("gx", "gy", "gz")),
        check_vma=False,
    )
```

profile of v0, /device:TPU:41, one launch (start us, length us, event | category | flops | bytes accessed | tf_op | source)
XLA Modules:
  0.0 181.9 jit_solution(772385167822043136)
XLA Ops:
  6.4 3.2 %multiply_reduce_fusion.10 = bf16[50,8,384]{2,1,0:T(8,128)(2,1)S(1)} fusion(f32[50,8,384]{2,1,0:T(8,128)S(1)} %convert_element_type.147, f32[50,50,384]{2,1,0:T(8,128)S(1)} %convert_element_type.146), kind=kLoop, calls=%fused_computation.24 | loop fusion | flops 15206400 | bytes 4761600 | tf_op jit(solution)/shard_map/reduce_sum | solution.py:17
  14.1 3.2 %collective-permute-start.4 = (bf16[50,8,64]{2,1,0:T(8,128)(2,1)S(1)}, bf16[50,8,64]{2,1,0:T(8,128)(2,1)S(1)}, u32[]{:S(2)}, u32[]{:S(2)}) collective-permute-start(bf16[50,8,64]{2,1,0:T(8,128)(2,1)S(1)} %select_bitcast_fusion.7), channel_id=1, source_target_pairs={{0,1},{1,2},{2,3},{4,5},{5,6},{6,7},{8,9},{9,10},{10,11},{12,13},{... | collective-permute-start | bytes 153608 | tf_op jit(solution)/shard_map/ppermute | solution.py:12
  18.1 3.1 %collective-permute-start.3 = (bf16[50,8,64]{2,1,0:T(8,128)(2,1)S(1)}, bf16[50,8,64]{2,1,0:T(8,128)(2,1)S(1)}, u32[]{:S(2)}, u32[]{:S(2)}) collective-permute-start(bf16[50,8,64]{2,1,0:T(8,128)(2,1)S(1)} %select_bitcast_fusion.8), channel_id=1, source_target_pairs={{4,0},{8,4},{12,8},{5,1},{9,5},{13,9},{6,2},{10,6},{14,10},{7,3},{... | collective-permute-start | bytes 153608 | tf_op jit(solution)/shard_map/ppermute | solution.py:12
  22.1 7.8 %collective-permute-start.2 = (bf16[50,8,64]{2,1,0:T(8,128)(2,1)S(1)}, bf16[50,8,64]{2,1,0:T(8,128)(2,1)S(1)}, u32[]{:S(2)}, u32[]{:S(2)}) collective-permute-start(bf16[50,8,64]{2,1,0:T(8,128)(2,1)S(1)} %select_bitcast_fusion.9), channel_id=1, source_target_pairs={{0,4},{4,8},{8,12},{1,5},{5,9},{9,13},{2,6},{6,10},{10,14},{3,7},{... | collective-permute-start | bytes 153608 | tf_op jit(solution)/shard_map/ppermute | solution.py:12
  30.9 3.1 %collective-permute-start = (bf16[50,8,128]{2,1,0:T(8,128)(2,1)S(1)}, bf16[50,8,128]{2,1,0:T(8,128)(2,1)S(1)}, u32[]{:S(2)}, u32[]{:S(2)}) collective-permute-start(bf16[50,8,128]{2,1,0:T(8,128)(2,1)S(1)} %select_bitcast_fusion.11), channel_id=1, source_target_pairs={{0,16},{16,32},{32,48},{48,64},{64,80},{80,96},{96,112},{112,128},... | collective-permute-start | bytes 307208 | tf_op jit(solution)/shard_map/ppermute | solution.py:12
  35.1 19.4 %fusion.14 = (bf16[1,50,50,384]{3,0,2,1:T(2,128)(2,1)S(1)}, bf16[1,50,50,384]{3,0,2,1:T(2,128)(2,1)S(1)}, bf16[1,50,50,384]{3,0,2,1:T(2,128)(2,1)S(1)}, bf16[1,50,50,384]{3,0,2,1:T(2,128)(2,1)S(1)}) fusion(bf16[4,50,50,384]{3,0,2,1:T(4,128)(2,1)} %param.15), kind=kLoop, calls=%fused_computation.98 | loop fusion | bytes 15360000 | tf_op jit(solution)/shard_map/slice | solution.py:63
  63.8 4.5 %collective-permute-start.1 = (bf16[50,8,128]{2,1,0:T(8,128)(2,1)S(1)}, bf16[50,8,128]{2,1,0:T(8,128)(2,1)S(1)}, u32[]{:S(2)}, u32[]{:S(2)}) collective-permute-start(bf16[50,8,128]{2,1,0:T(8,128)(2,1)S(1)} %select_bitcast_fusion.10), channel_id=1, source_target_pairs={{16,0},{32,16},{48,32},{64,48},{80,64},{96,80},{112,96},{128,112},... | collective-permute-start | bytes 307208 | tf_op jit(solution)/shard_map/ppermute | solution.py:12
  72.9 3.9 %gather_fusion.6 = bf16[1536,50,8]{1,2,0:T(8,128)(2,1)S(1)} fusion(bf16[50,8,896]{0,1,2:T(8,128)(2,1)} %copy.117, s32[2048]{0:T(1024)S(1)} %pad_clamp_fusion), kind=kCustom, calls=%fused_computation.2.clone | custom fusion | bytes 2463744 | tf_op jit(solution)/shard_map/jit(_take)/gather | solution.py:59
  76.8 5.6 %broadcast_select_fusion = bf16[1536,50,8]{1,2,0:T(8,128)(2,1)S(1)} fusion(bf16[1536,50,8]{1,2,0:T(8,128)(2,1)S(1)} %gather_fusion.6, pred[1536]{0:T(1024)(128)(4,1)S(1)} %compare_and_fusion), kind=kLoop, calls=%fused_computation.25 | loop fusion | flops 614400 | bytes 2459136 | tf_op jit(solution)/shard_map/jit(_take)/select_n | solution.py:59
  85.3 7.1 %multiply_reduce_fusion.8 = f32[50,8,384]{2,1,0:T(8,128)S(1)} fusion(f32[50,8,384]{2,1,0:T(8,128)S(1)} %fusion.12, f32[50,50,384]{2,1,0:T(8,128)} %fusion.2), kind=kLoop, calls=%fused_computation.22 | loop fusion | flops 15206400 | bytes 5068800 | tf_op jit(solution)/shard_map/reduce_sum | solution.py:17
  92.4 5.8 %multiply_reduce_fusion.7 = f32[50,8,384]{2,1,0:T(8,128)S(1)} fusion(f32[50,8,384]{2,1,0:T(8,128)S(1)} %fusion.11, f32[50,50,384]{2,1,0:T(8,128)} %fusion.1), kind=kLoop, calls=%fused_computation.21 | loop fusion | flops 15206400 | bytes 5068800 | tf_op jit(solution)/shard_map/reduce_sum | solution.py:17
  98.3 4.0 %multiply_reduce_fusion.9 = f32[50,8,384]{2,1,0:T(8,128)S(1)} fusion(f32[50,8,384]{2,1,0:T(8,128)S(1)} %fusion.13, f32[50,50,384]{2,1,0:T(8,128)S(1)} %bitcast.109), kind=kLoop, calls=%fused_computation.23 | loop fusion | flops 15206400 | bytes 5068800 | tf_op jit(solution)/shard_map/reduce_sum | solution.py:17
  102.3 4.0 %multiply_reduce_fusion.6 = f32[50,8,384]{2,1,0:T(8,128)S(1)} fusion(f32[50,8,384]{2,1,0:T(8,128)S(1)} %fusion.10, f32[50,50,384]{2,1,0:T(8,128)S(1)} %bitcast.113), kind=kLoop, calls=%fused_computation.20 | loop fusion | flops 15206400 | bytes 5068800 | tf_op jit(solution)/shard_map/reduce_sum | solution.py:17
  106.6 3.2 %multiply_reduce_fusion.5 = bf16[50,8,384]{2,1,0:T(8,128)(2,1)S(1)} fusion(f32[50,8,384]{2,1,0:T(8,128)S(1)} %fusion.4, f32[50,50,384]{2,1,0:T(8,128)S(1)} %bitcast.103), kind=kLoop, calls=%fused_computation.19 | loop fusion | flops 15206400 | bytes 4761600 | tf_op jit(solution)/shard_map/reduce_sum | solution.py:17
  116.9 3.2 %collective-permute-start.10 = (bf16[50,8,64]{2,1,0:T(8,128)(2,1)S(1)}, bf16[50,8,64]{2,1,0:T(8,128)(2,1)S(1)}, u32[]{:S(2)}, u32[]{:S(2)}) collective-permute-start(bf16[50,8,64]{2,1,0:T(8,128)(2,1)S(1)} %select_bitcast_fusion.1), channel_id=1, source_target_pairs={{0,1},{1,2},{2,3},{4,5},{5,6},{6,7},{8,9},{9,10},{10,11},{12,13},{... | collective-permute-start | bytes 153608 | tf_op jit(solution)/shard_map/ppermute | solution.py:12
  125.5 5.2 %collective-permute-start.7 = (bf16[50,8,128]{2,1,0:T(8,128)(2,1)S(1)}, bf16[50,8,128]{2,1,0:T(8,128)(2,1)S(1)}, u32[]{:S(2)}, u32[]{:S(2)}) collective-permute-start(bf16[50,8,128]{2,1,0:T(8,128)(2,1)S(1)} %select_bitcast_fusion.4), channel_id=1, source_target_pairs={{16,0},{32,16},{48,32},{64,48},{80,64},{96,80},{112,96},{128,112},... | collective-permute-start | bytes 307208 | tf_op jit(solution)/shard_map/ppermute | solution.py:12
  130.8 8.1 %collective-permute-start.8 = (bf16[50,8,64]{2,1,0:T(8,128)(2,1)S(1)}, bf16[50,8,64]{2,1,0:T(8,128)(2,1)S(1)}, u32[]{:S(2)}, u32[]{:S(2)}) collective-permute-start(bf16[50,8,64]{2,1,0:T(8,128)(2,1)S(1)} %select_bitcast_fusion.3), channel_id=1, source_target_pairs={{0,4},{4,8},{8,12},{1,5},{5,9},{9,13},{2,6},{6,10},{10,14},{3,7},{... | collective-permute-start | bytes 153608 | tf_op jit(solution)/shard_map/ppermute | solution.py:12
  143.5 3.9 %gather_fusion.13 = bf16[1536,50,8]{1,2,0:T(8,128)(2,1)S(1)} fusion(bf16[50,8,896]{0,1,2:T(8,128)(2,1)} %copy.138, s32[2048]{0:T(1024)S(1)} %pad_clamp_fusion), kind=kCustom, calls=%fused_computation.13.clone | custom fusion | bytes 2463744 | tf_op jit(solution)/shard_map/jit(_take)/gather | solution.py:59
  147.4 5.6 %broadcast_select_fusion.1 = bf16[1536,50,8]{1,2,0:T(8,128)(2,1)S(1)} fusion(bf16[1536,50,8]{1,2,0:T(8,128)(2,1)S(1)} %gather_fusion.13, pred[1536]{0:T(1024)(128)(4,1)S(1)} %compare_and_fusion), kind=kLoop, calls=%fused_computation.26 | loop fusion | flops 614400 | bytes 2459136 | tf_op jit(solution)/shard_map/jit(_take)/select_n | solution.py:59
  156.5 7.1 %multiply_reduce_fusion.2 = f32[50,8,384]{2,1,0:T(8,128)S(1)} fusion(f32[50,8,384]{2,1,0:T(8,128)S(1)} %get-tuple-element.45, f32[50,50,384]{2,1,0:T(8,128)} %fusion.1), kind=kLoop, calls=%fused_computation.16 | loop fusion | flops 15206400 | bytes 5068800 | tf_op jit(solution)/shard_map/reduce_sum | solution.py:17
  163.6 5.8 %multiply_reduce_fusion.1 = f32[50,8,384]{2,1,0:T(8,128)S(1)} fusion(f32[50,8,384]{2,1,0:T(8,128)S(1)} %get-tuple-element.44, f32[50,50,384]{2,1,0:T(8,128)} %fusion), kind=kLoop, calls=%fused_computation.15 | loop fusion | flops 15206400 | bytes 5068800 | tf_op jit(solution)/shard_map/reduce_sum | solution.py:17
  169.5 4.0 %multiply_reduce_fusion.4 = f32[50,8,384]{2,1,0:T(8,128)S(1)} fusion(f32[50,8,384]{2,1,0:T(8,128)S(1)} %get-tuple-element.47, f32[50,50,384]{2,1,0:T(8,128)S(1)} %bitcast.111), kind=kLoop, calls=%fused_computation.18 | loop fusion | flops 15206400 | bytes 5068800 | tf_op jit(solution)/shard_map/reduce_sum | solution.py:17
  173.6 4.0 %multiply_reduce_fusion.3 = f32[50,8,384]{2,1,0:T(8,128)S(1)} fusion(f32[50,8,384]{2,1,0:T(8,128)S(1)} %get-tuple-element.46, f32[50,50,384]{2,1,0:T(8,128)S(1)} %bitcast.107), kind=kLoop, calls=%fused_computation.17 | loop fusion | flops 15206400 | bytes 5068800 | tf_op jit(solution)/shard_map/reduce_sum | solution.py:17
  177.9 3.2 %multiply_reduce_fusion = bf16[50,8,384]{2,1,0:T(8,128)(2,1)S(1)} fusion(f32[50,8,384]{2,1,0:T(8,128)S(1)} %fusion.5, f32[50,50,384]{2,1,0:T(8,128)S(1)} %bitcast.105), kind=kLoop, calls=%fused_computation.14 | loop fusion | flops 15206400 | bytes 4761600 | tf_op jit(solution)/shard_map/reduce_sum | solution.py:17
  (145 shorter events, 52.2 us)
Async XLA Ops:
  6.4 23.5 %copy-start.6 = (s32[1,2,128]{2,1,0:T(2,128)S(1)}, s32[1,2,128]{2,1,0:T(2,128)}, u32[]{:S(2)}) copy-start(s32[1,2,128]{2,1,0:T(2,128)} %param.20) | copy-start | bytes 3076
  6.4 27.7 %copy-start.4 = (s32[4,384]{1,0:T(4,128)S(1)}, s32[4,384]{1,0:T(4,128)}, u32[]{:S(2)}) copy-start(s32[4,384]{1,0:T(4,128)} %param.18) | copy-start | bytes 18436
  6.4 27.7 %copy-start.5 = (s32[4,384]{1,0:T(4,128)S(1)}, s32[4,384]{1,0:T(4,128)}, u32[]{:S(2)}) copy-start(s32[4,384]{1,0:T(4,128)} %param.19) | copy-start | bytes 18436
  11.1 52.6 %collective-permute-start.5 = (bf16[50,8,64]{2,1,0:T(8,128)(2,1)S(1)}, bf16[50,8,64]{2,1,0:T(8,128)(2,1)S(1)}, u32[]{:S(2)}, u32[]{:S(2)}) collective-permute-start(bf16[50,8,64]{2,1,0:T(8,128)(2,1)S(1)} %select_bitcast_fusion.6), channel_id=1, source_target_pairs={{1,0},{2,1},{3,2},{5,4},{6,5},{7,6},{9,8},{10,9},{11,10},{13,12},{... | collective-permute-start | bytes 153608 | tf_op jit(solution)/shard_map/ppermute | solution.py:12
  14.1 54.2 %collective-permute-start.4 = (bf16[50,8,64]{2,1,0:T(8,128)(2,1)S(1)}, bf16[50,8,64]{2,1,0:T(8,128)(2,1)S(1)}, u32[]{:S(2)}, u32[]{:S(2)}) collective-permute-start(bf16[50,8,64]{2,1,0:T(8,128)(2,1)S(1)} %select_bitcast_fusion.7), channel_id=1, source_target_pairs={{0,1},{1,2},{2,3},{4,5},{5,6},{6,7},{8,9},{9,10},{10,11},{12,13},{... | collective-permute-start | bytes 153608 | tf_op jit(solution)/shard_map/ppermute | solution.py:12
  18.1 50.1 %collective-permute-start.3 = (bf16[50,8,64]{2,1,0:T(8,128)(2,1)S(1)}, bf16[50,8,64]{2,1,0:T(8,128)(2,1)S(1)}, u32[]{:S(2)}, u32[]{:S(2)}) collective-permute-start(bf16[50,8,64]{2,1,0:T(8,128)(2,1)S(1)} %select_bitcast_fusion.8), channel_id=1, source_target_pairs={{4,0},{8,4},{12,8},{5,1},{9,5},{13,9},{6,2},{10,6},{14,10},{7,3},{... | collective-permute-start | bytes 153608 | tf_op jit(solution)/shard_map/ppermute | solution.py:12
  22.1 46.1 %collective-permute-start.2 = (bf16[50,8,64]{2,1,0:T(8,128)(2,1)S(1)}, bf16[50,8,64]{2,1,0:T(8,128)(2,1)S(1)}, u32[]{:S(2)}, u32[]{:S(2)}) collective-permute-start(bf16[50,8,64]{2,1,0:T(8,128)(2,1)S(1)} %select_bitcast_fusion.9), channel_id=1, source_target_pairs={{0,4},{4,8},{8,12},{1,5},{5,9},{9,13},{2,6},{6,10},{10,14},{3,7},{... | collective-permute-start | bytes 153608 | tf_op jit(solution)/shard_map/ppermute | solution.py:12
  30.9 37.3 %collective-permute-start = (bf16[50,8,128]{2,1,0:T(8,128)(2,1)S(1)}, bf16[50,8,128]{2,1,0:T(8,128)(2,1)S(1)}, u32[]{:S(2)}, u32[]{:S(2)}) collective-permute-start(bf16[50,8,128]{2,1,0:T(8,128)(2,1)S(1)} %select_bitcast_fusion.11), channel_id=1, source_target_pairs={{0,16},{16,32},{32,48},{48,64},{64,80},{80,96},{96,112},{112,128},... | collective-permute-start | bytes 307208 | tf_op jit(solution)/shard_map/ppermute | solution.py:12
  63.8 5.9 %collective-permute-start.1 = (bf16[50,8,128]{2,1,0:T(8,128)(2,1)S(1)}, bf16[50,8,128]{2,1,0:T(8,128)(2,1)S(1)}, u32[]{:S(2)}, u32[]{:S(2)}) collective-permute-start(bf16[50,8,128]{2,1,0:T(8,128)(2,1)S(1)} %select_bitcast_fusion.10), channel_id=1, source_target_pairs={{16,0},{32,16},{48,32},{64,48},{80,64},{96,80},{112,96},{128,112},... | collective-permute-start | bytes 307208 | tf_op jit(solution)/shard_map/ppermute | solution.py:12
  85.2 13.0 %slice-start.6 = ((s8[4300800]{0:T(1024)(128)(4,1)}), s8[4194304]{0:T(1024)(128)(4,1)S(1)}, s32[]{:S(2)}) async-start(s8[4300800]{0:T(1024)(128)(4,1)} %bitcast.108), calls=%async_computation.6 | async-start | bytes 8388608
  85.3 12.9 %slice-start.7 = ((s8[4300800]{0:T(1024)(128)(4,1)}), s8[106496]{0:T(1024)(128)(4,1)S(1)}, s32[]{:S(2)}) async-start(s8[4300800]{0:T(1024)(128)(4,1)} %bitcast.108), calls=%async_computation.7 | async-start | bytes 212992
  85.3 17.0 %slice-start.10 = ((s8[4300800]{0:T(1024)(128)(4,1)}), s8[4194304]{0:T(1024)(128)(4,1)S(1)}, s32[]{:S(2)}) async-start(s8[4300800]{0:T(1024)(128)(4,1)} %bitcast.112), calls=%async_computation.10 | async-start | bytes 8388608
  92.4 9.9 %slice-start.11 = ((s8[4300800]{0:T(1024)(128)(4,1)}), s8[106496]{0:T(1024)(128)(4,1)S(1)}, s32[]{:S(2)}) async-start(s8[4300800]{0:T(1024)(128)(4,1)} %bitcast.112), calls=%async_computation.11 | async-start | bytes 212992
  114.6 16.1 %collective-permute-start.11 = (bf16[50,8,64]{2,1,0:T(8,128)(2,1)S(1)}, bf16[50,8,64]{2,1,0:T(8,128)(2,1)S(1)}, u32[]{:S(2)}, u32[]{:S(2)}) collective-permute-start(bf16[50,8,64]{2,1,0:T(8,128)(2,1)S(1)} %select_bitcast_fusion), channel_id=1, source_target_pairs={{1,0},{2,1},{3,2},{5,4},{6,5},{7,6},{9,8},{10,9},{11,10},{13,12},{... | collective-permute-start | bytes 153608 | tf_op jit(solution)/shard_map/ppermute | solution.py:12
  116.9 21.9 %collective-permute-start.10 = (bf16[50,8,64]{2,1,0:T(8,128)(2,1)S(1)}, bf16[50,8,64]{2,1,0:T(8,128)(2,1)S(1)}, u32[]{:S(2)}, u32[]{:S(2)}) collective-permute-start(bf16[50,8,64]{2,1,0:T(8,128)(2,1)S(1)} %select_bitcast_fusion.1), channel_id=1, source_target_pairs={{0,1},{1,2},{2,3},{4,5},{5,6},{6,7},{8,9},{9,10},{10,11},{12,13},{... | collective-permute-start | bytes 153608 | tf_op jit(solution)/shard_map/ppermute | solution.py:12
  120.3 18.5 %collective-permute-start.9 = (bf16[50,8,64]{2,1,0:T(8,128)(2,1)S(1)}, bf16[50,8,64]{2,1,0:T(8,128)(2,1)S(1)}, u32[]{:S(2)}, u32[]{:S(2)}) collective-permute-start(bf16[50,8,64]{2,1,0:T(8,128)(2,1)S(1)} %select_bitcast_fusion.2), channel_id=1, source_target_pairs={{4,0},{8,4},{12,8},{5,1},{9,5},{13,9},{6,2},{10,6},{14,10},{7,3},{... | collective-permute-start | bytes 153608 | tf_op jit(solution)/shard_map/ppermute | solution.py:12
  122.9 17.3 %collective-permute-start.6 = (bf16[50,8,128]{2,1,0:T(8,128)(2,1)S(1)}, bf16[50,8,128]{2,1,0:T(8,128)(2,1)S(1)}, u32[]{:S(2)}, u32[]{:S(2)}) collective-permute-start(bf16[50,8,128]{2,1,0:T(8,128)(2,1)S(1)} %select_bitcast_fusion.5), channel_id=1, source_target_pairs={{0,16},{16,32},{32,48},{48,64},{64,80},{80,96},{96,112},{112,128},... | collective-permute-start | bytes 307208 | tf_op jit(solution)/shard_map/ppermute | solution.py:12
  125.5 14.7 %collective-permute-start.7 = (bf16[50,8,128]{2,1,0:T(8,128)(2,1)S(1)}, bf16[50,8,128]{2,1,0:T(8,128)(2,1)S(1)}, u32[]{:S(2)}, u32[]{:S(2)}) collective-permute-start(bf16[50,8,128]{2,1,0:T(8,128)(2,1)S(1)} %select_bitcast_fusion.4), channel_id=1, source_target_pairs={{16,0},{32,16},{48,32},{64,48},{80,64},{96,80},{112,96},{128,112},... | collective-permute-start | bytes 307208 | tf_op jit(solution)/shard_map/ppermute | solution.py:12
  130.8 9.5 %collective-permute-start.8 = (bf16[50,8,64]{2,1,0:T(8,128)(2,1)S(1)}, bf16[50,8,64]{2,1,0:T(8,128)(2,1)S(1)}, u32[]{:S(2)}, u32[]{:S(2)}) collective-permute-start(bf16[50,8,64]{2,1,0:T(8,128)(2,1)S(1)} %select_bitcast_fusion.3), channel_id=1, source_target_pairs={{0,4},{4,8},{8,12},{1,5},{5,9},{9,13},{2,6},{6,10},{10,14},{3,7},{... | collective-permute-start | bytes 153608 | tf_op jit(solution)/shard_map/ppermute | solution.py:12
  155.1 14.4 %slice-start.8 = ((s8[4300800]{0:T(1024)(128)(4,1)}), s8[106496]{0:T(1024)(128)(4,1)S(1)}, s32[]{:S(2)}) async-start(s8[4300800]{0:T(1024)(128)(4,1)} %bitcast.110), calls=%async_computation.8 | async-start | bytes 212992
  156.4 13.0 %copy-start.3 = (bf16[50,8,1,384]{3,1,0,2:T(8,128)(2,1)S(1)}, bf16[50,8,1,384]{3,1,0,2:T(8,128)(2,1)}, u32[]{:S(2)}) copy-start(bf16[50,8,1,384]{3,1,0,2:T(8,128)(2,1)} %copy.157) | copy-start | bytes 921604
  156.4 13.1 %slice-start.9 = ((s8[4300800]{0:T(1024)(128)(4,1)}), s8[4194304]{0:T(1024)(128)(4,1)S(1)}, s32[]{:S(2)}) async-start(s8[4300800]{0:T(1024)(128)(4,1)} %bitcast.110), calls=%async_computation.9 | async-start | bytes 8388608
  156.4 17.1 %slice-start.4 = ((s8[4300800]{0:T(1024)(128)(4,1)}), s8[4194304]{0:T(1024)(128)(4,1)S(1)}, s32[]{:S(2)}) async-start(s8[4300800]{0:T(1024)(128)(4,1)} %bitcast.106), calls=%async_computation.4 | async-start | bytes 8388608
  163.6 10.0 %slice-start.5 = ((s8[4300800]{0:T(1024)(128)(4,1)}), s8[106496]{0:T(1024)(128)(4,1)S(1)}, s32[]{:S(2)}) async-start(s8[4300800]{0:T(1024)(128)(4,1)} %bitcast.106), calls=%async_computation.5 | async-start | bytes 212992
  (7 other events, 39.4 us)
where the time goes:
time: 183 us; the launch traced here: 182 us
  other arithmetic  77.6 us (42%)
  local copies, waits for them, and re-layouts  53 us (29%)
  starting transfers between devices  46.8 us (26%)
  waiting for transfers between devices  2.86 us (2%)
    reduce_sum x11, other arithmetic, block_apply(): return jnp.sum(product, axis=1)  51.5 us
    ppermute x12, starting transfers between devices, passed_along(): return lax.ppermute(shard, axis, pairs)  46.8 us
    slice x1, local copies, waits for them, and re-layouts, shards(): coupling = coupling + block_apply(face_blocks[face], beside)  19.4 us
    select_n x3, other arithmetic, shards(): jnp.take(gathered, flat_lookup, axis=2)  11.2 us
    convert_element_type x5, other arithmetic, block_apply(): blocks[:, :, None, :].astype(jnp.float32)  11.1 us
    gather x2, local copies, waits for them, and re-layouts, shards(): jnp.take(gathered, flat_lookup, axis=2)  7.76 us
    unnamed x46, local copies, waits for them, and re-layouts  7.5 us
    concatenate x4, local copies, waits for them, and re-layouts, shards(): gathered = jnp.concatenate([adjoint] + received, axis=2)  6.47 us
  transfers between devices with their start and end apart: 12, of which 2 were waited for; matrix products, arithmetic and copies ran while one was open for 19% of the time, Pallas kernels for 0%

commit v1 on v0

v1 whole, which is shorter than its diff:
```python
import jax
import jax.numpy as jnp
from jax import lax
from jax.experimental import pallas as pl
from jax.experimental.pallas import tpu as pltpu
from jax.sharding import PartitionSpec as P

BF = jnp.bfloat16
F32 = jnp.float32
I32 = jnp.int32
SWEEPS = 2
NB = 50
NF = 8
FACES = 4
ROWS = NB * NF
E = 384
L = 128
T = E // L
FR = 208
XR = 64
HALO = 512
SRC = E + HALO
PACK = 208
DIRECTIONS = (("gx", 1), ("gx", -1), ("gy", 1), ("gy", -1), ("gz", 1), ("gz", -1))
OFFSETS = (0, E, E + 128, E + 256, E + 320, E + 384, E + 448)
MESH = pl.DeviceIdType.MESH
FACE_GROUPS = ((0, 1, 2, 3), (4, 5, 6), (7, 8, 9), (10, 11, 12))
INV_GROUPS = ((0, 1, 2, 3),)


def at16(index):
    return pl.ds(pl.multiple_of(index * 16, 16), 16)


def whole_tiles(get, count):
    value = jnp.concatenate([get(m) for m in range(count)], axis=0)
    return [value[16 * m : 16 * m + 16] for m in range(count)]


def kernel(
    inv_hbm, face_hbm, load_ref, live_ref, kind_ref, slot_ref, sx_ref, syz_ref, out_ref,
    faces, inverse, adj, wide_x, vec_x, wide_b, vec_b, pick_send, pick, send_x, send_yz, recv_x, recv_yz,
    block_sem, send_sem, recv_sem,
):
    position = {axis: lax.axis_index(axis) for axis in ("gx", "gy", "gz")}
    sends, receives = [], []
    for axis, step in DIRECTIONS:
        length = lax.axis_size(axis)
        ahead, behind = position[axis] + step, position[axis] - step
        sends.append((ahead >= 0) & (ahead < length))
        receives.append((behind >= 0) & (behind < length))

    def block_copy(t):
        return pltpu.make_async_copy(
            inv_hbm.at[:, :, pl.ds(L * t, L)], inverse.at[t, :, pl.ds(0, NB), :], block_sem.at[t]
        )

    def face_copy(t):
        return pltpu.make_async_copy(
            face_hbm.reshape(NB, NB * FACES, E).at[:, :, pl.ds(L * t, L)],
            faces.at[t, :, pl.ds(0, NB * FACES), :],
            block_sem.at[T + t],
        )

    for t in range(T):
        block_copy(t).start()
    for t in range(T):
        face_copy(t).start()

    for d in range(6):

        @pl.when(jnp.logical_not(receives[d]))
        def _(d=d):
            for s in range(SWEEPS):
                if d < 2:
                    recv_x[s, d] = jnp.zeros((ROWS, L), BF)
                else:
                    recv_yz[s, d - 2] = jnp.zeros((PACK, L), BF)

    barrier = pltpu.get_barrier_semaphore()
    for d, (axis, step) in enumerate(DIRECTIONS):

        @pl.when(sends[d])
        def _(axis=axis, step=step):
            pl.semaphore_signal(
                barrier, inc=1, device_id={axis: position[axis] + step}, device_id_type=MESH
            )

    def halo_copy(s, d):
        axis, step = DIRECTIONS[d]
        source, target = (send_x, recv_x) if d < 2 else (send_yz, recv_yz)
        at = d if d < 2 else d - 2
        beside = jnp.clip(position[axis] + step, 0, lax.axis_size(axis) - 1)
        return pltpu.make_async_remote_copy(
            src_ref=source.at[s, at],
            dst_ref=target.at[s, at],
            send_sem=send_sem.at[s, d],
            recv_sem=recv_sem.at[s, d],
            device_id={axis: beside},
            device_id_type=MESH,
        )

    live = live_ref[0]
    lane = lax.broadcasted_iota(I32, (16, L), 1)
    low = lane < 64
    group_sum = (
        lax.shift_right_logical(lax.broadcasted_iota(I32, (16, 256), 1), 4)
        == lax.broadcasted_iota(I32, (16, 256), 0)
    )
    group_sum = group_sum.astype(F32).astype(BF)

    def pad_tile(t, _):
        for k in range(NF):
            wide_x[t, k * XR + 48 : k * XR + 64, :] = jnp.zeros((16, L), F32)
            wide_b[t, k * FR + 200 : k * FR + 208, :] = jnp.zeros((8, L), F32)

        def pad_row(i, _):
            faces[t, i, 200:208, :] = jnp.zeros((8, L), BF)
            return 0

        return lax.fori_loop(0, NB, pad_row, 0)

    lax.fori_loop(0, T, pad_tile, 0)

    def lanes(t):
        return pl.ds(pl.multiple_of(t * L, L), L)

    def scatter_x(t, i2, value):
        for half in range(2):
            wide_x[t, pl.ds(2 * i2 + half, NF, stride=XR), :] = value[8 * half : 8 * half + 8]

    def narrow_x(t):
        for k in range(NF):
            for m in range(XR // 16):
                r = k * XR + 16 * m
                vec_x[t, k, 16 * m : 16 * m + 16, :] = wide_x[t, r : r + 16, :].astype(BF)

    def contract(blocks, vectors, count, groups):
        tiles = [whole_tiles(lambda m, half=half: blocks(half, m), count) for half in range(2)]
        sums = {}
        for k in range(NF):
            vector = whole_tiles(lambda m, k=k: vectors(k, m), count)
            for g, members in enumerate(groups):
                for half in range(2):
                    total = None
                    for m in members:
                        product = tiles[half][m] * vector[m]
                        total = product if total is None else total + product
                    sums[g, half, k] = total
        stacked = [
            sums[g, half, k] for g in range(len(groups)) for half in range(2) for k in range(NF)
        ]
        return jnp.dot(
            jnp.concatenate([group_sum] * len(groups), axis=1),
            jnp.concatenate(stacked, axis=0),
            preferred_element_type=F32,
        )

    def load_rows(t, i2):
        return load_ref[at16(i2), lanes(t)].astype(F32)

    def apply_inverse(t, s):
        alive = (lane + t * L) < live

        def body(i2, _):
            total = contract(
                lambda half, m: inverse[t, 2 * i2 + half, 16 * m : 16 * m + 16, :],
                lambda k, m: vec_x[t, k, 16 * m : 16 * m + 16, :],
                XR // 16,
                INV_GROUPS,
            )
            adj[s, at16(i2), lanes(t)] = jnp.where(alive, total, 0.0).astype(BF)
            return 0

        lax.fori_loop(0, NB // 2, body, 0, unroll=5)

    def apply_faces(t):
        def body(i2, _):
            total = contract(
                lambda half, m: faces[t, 2 * i2 + half, 16 * m : 16 * m + 16, :],
                lambda k, m: vec_b[t, k, 16 * m : 16 * m + 16, :],
                FR // 16,
                FACE_GROUPS,
            )
            scatter_x(t, i2, load_rows(t, i2) - total)
            return 0

        lax.fori_loop(0, NB // 2, body, 0, unroll=5)

    lists = [sx_ref[0, 0:1, :], sx_ref[0, 1:2, :]]
    for pair in range(2):
        lists.append(
            jnp.concatenate(
                [syz_ref[0, 2 * pair : 2 * pair + 1, :], syz_ref[0, 2 * pair + 1 : 2 * pair + 2, :]],
                axis=1,
            )
        )
    for c in range(4):

        def fill_send(b, _, c=c):
            row = lax.broadcasted_iota(I32, (16, L), 0) + b * 16
            pick_send[at16(b), c * L : (c + 1) * L] = jnp.where(row == lists[c], 1.0, 0.0).astype(BF)
            return 0

        lax.fori_loop(0, E // 16, fill_send, 0, unroll=8)

    def load_tile(i2, _):
        for t in range(T):
            scatter_x(t, i2, load_rows(t, i2))
        return 0

    lax.fori_loop(0, NB // 2, load_tile, 0)
    for t in range(T):
        block_copy(t).wait()

    def first(t, _):
        def clear(i, _):
            tail = inverse[t, i, 48:64, :].astype(F32)
            row = lax.broadcasted_iota(I32, (16, L), 0)
            inverse[t, i, 48:64, :] = jnp.where(row < 2, tail, 0.0).astype(BF)
            return 0

        lax.fori_loop(0, NB, clear, 0, unroll=5)
        narrow_x(t)
        apply_inverse(t, 0)
        return 0

    lax.fori_loop(0, T, first, 0)

    def send_halo(s):
        for pair in (0, 1):
            both = jnp.dot(
                adj[s, :, 0:E], pick_send[:, (2 + pair) * L : (3 + pair) * L], preferred_element_type=F32
            )
            for r in range(PACK // 16):
                upper = both[16 * r : 16 * r + 16]
                if PACK + 16 * r < ROWS:
                    lower = both[PACK + 16 * r : PACK + 16 * r + 16]
                else:
                    lower = jnp.zeros((16, L), F32)
                ahead = jnp.where(low, upper, pltpu.roll(lower, 64, 1))
                behind = jnp.where(low, pltpu.roll(upper, 64, 1), lower)
                send_yz[s, 2 * pair, 16 * r : 16 * r + 16, :] = ahead.astype(BF)
                send_yz[s, 2 * pair + 1, 16 * r : 16 * r + 16, :] = behind.astype(BF)
            if pair == 0:
                start_halo(s, (2, 3))
                for d in range(2):
                    send_x[s, d] = jnp.dot(
                        adj[s, :, 0:E], pick_send[:, d * L : (d + 1) * L], preferred_element_type=F32
                    ).astype(BF)
                start_halo(s, (0, 1))
        start_halo(s, (4, 5))

    def start_halo(s, directions):
        for d in directions:

            @pl.when(sends[d])
            def _(d=d):
                halo_copy(s, d).start()

    def take_halo(s):
        for d in range(6):

            @pl.when(receives[d])
            def _(d=d):
                halo_copy(s, d).wait_recv()

        for d in range(2):
            adj[s, :, E + d * L : E + (d + 1) * L] = recv_x[s, d]
        for pair in range(2):
            column = E + (2 + pair) * L
            for r in range(PACK // 16):
                ahead = recv_yz[s, 2 * pair, 16 * r : 16 * r + 16, :].astype(F32)
                behind = recv_yz[s, 2 * pair + 1, 16 * r : 16 * r + 16, :].astype(F32)
                upper = jnp.where(low, ahead, pltpu.roll(behind, 64, 1))
                adj[s, 16 * r : 16 * r + 16, column : column + L] = upper.astype(BF)
                if PACK + 16 * r < ROWS:
                    lower = jnp.where(low, pltpu.roll(ahead, 64, 1), behind)
                    adj[s, PACK + 16 * r : PACK + 16 * r + 16, column : column + L] = lower.astype(BF)

    def gather_faces(t, s):
        for f in range(0, FACES, 2):
            picked = jnp.dot(adj[s], pick[t, :, f * L : (f + 2) * L], preferred_element_type=F32)
            for j in range(NB):
                for g in range(2):
                    rows = pl.ds(FACES * j + f + g, NF, stride=FR)
                    wide_b[t, rows, :] = picked[8 * j : 8 * j + 8, g * L : (g + 1) * L]

        def narrow(k, _):
            for m in range(FR // 16):
                r = pl.ds(pl.multiple_of(k * FR + 16 * m, 16), 16)
                vec_b[t, k, 16 * m : 16 * m + 16, :] = wide_b[t, r, :].astype(BF)
            return 0

        lax.fori_loop(0, NF, narrow, 0)

    pl.semaphore_wait(barrier, sum(jnp.where(there, 1, 0) for there in sends))
    send_halo(0)

    kind = kind_ref[...]
    look = jnp.where(kind == 0, -1, slot_ref[...])
    for d in range(7):
        look = look + jnp.where(kind == d + 1, OFFSETS[d], 0)
    for t in range(T):
        for f in range(FACES):
            wanted = look[f : f + 1, t * L : (t + 1) * L]

            def fill(b, _, t=t, f=f, wanted=wanted):
                row = lax.broadcasted_iota(I32, (16, L), 0) + b * 16
                pick[t, at16(b), f * L : (f + 1) * L] = jnp.where(row == wanted, 1.0, 0.0).astype(BF)
                return 0

            lax.fori_loop(0, SRC // 16, fill, 0, unroll=8)
    for t in range(T):
        face_copy(t).wait()

    for s in range(SWEEPS):
        take_halo(s)

        def sweep(t, _, s=s):
            gather_faces(t, s)
            apply_faces(t)
            narrow_x(t)
            apply_inverse(t, s + 1)
            return 0

        lax.fori_loop(0, T, sweep, 0)
        if s + 1 < SWEEPS:
            send_halo(s + 1)
    out_ref[...] = adj[SWEEPS, :, 0:E]
    for s in range(SWEEPS):
        for d in range(6):

            @pl.when(sends[d])
            def _(s=s, d=d):
                halo_copy(s, d).wait_send()


def shards(inverse_blocks, face_blocks, load_vector, live_counts, nbr_kind, nbr_slot, send_x, send_yz):
    by_row = jnp.transpose(face_blocks, (1, 2, 0, 3))
    anywhere = pl.BlockSpec(memory_space=pl.ANY)
    on_core = pl.BlockSpec(memory_space=pltpu.VMEM)
    scalar = pl.BlockSpec(memory_space=pltpu.SMEM)
    result = pl.pallas_call(
        kernel,
        out_shape=jax.ShapeDtypeStruct((ROWS, E), BF),
        in_specs=[anywhere, anywhere, on_core, scalar, on_core, on_core, on_core, on_core],
        out_specs=on_core,
        scratch_shapes=[
            pltpu.VMEM((T, NB, FR, L), BF),
            pltpu.VMEM((T, NB, XR, L), BF),
            pltpu.VMEM((SWEEPS + 1, ROWS, SRC), BF),
            pltpu.VMEM((T, NF * XR, L), F32),
            pltpu.VMEM((T, NF, XR, L), BF),
            pltpu.VMEM((T, NF * FR, L), F32),
            pltpu.VMEM((T, NF, FR, L), BF),
            pltpu.VMEM((E, HALO), BF),
            pltpu.VMEM((T, SRC, FACES * L), BF),
            pltpu.VMEM((SWEEPS, 2, ROWS, L), BF),
            pltpu.VMEM((SWEEPS, 4, PACK, L), BF),
            pltpu.VMEM((SWEEPS, 2, ROWS, L), BF),
            pltpu.VMEM((SWEEPS, 4, PACK, L), BF),
            pltpu.SemaphoreType.DMA((2 * T,)),
            pltpu.SemaphoreType.DMA((SWEEPS, 6)),
            pltpu.SemaphoreType.DMA((SWEEPS, 6)),
        ],
        compiler_params=pltpu.CompilerParams(
            vmem_limit_bytes=60 * 2**20, collective_id=0, has_side_effects=True
        ),
    )(
        inverse_blocks, by_row, load_vector.reshape(ROWS, E), live_counts,
        nbr_kind, nbr_slot, send_x, send_yz,
    )
    return result.reshape(NB, NF, E)


def solution(mesh):
    elements = ("gx", "gy", "gz")
    placed = (
        P(None, None, elements),
        P(None, None, None, elements),
        P(None, None, elements),
        P(elements),
        P(None, elements),
        P(None, elements),
        P(elements, None, None),
        P(elements, None, None),
    )
    return jax.shard_map(
        shards, mesh=mesh, in_specs=placed, out_specs=P(None, None, elements), check_vma=False
    )
```

time: 183 us -> 49.9 us (0.27)
  other arithmetic: 77.6 us -> 0 us
  local copies, waits for them, and re-layouts: 53 us -> 1.71 us
  Pallas kernels: 0 us -> 47.4 us
  starting transfers between devices: 46.8 us -> 0 us
  waiting for transfers between devices: 2.86 us -> 0 us
    reduce_sum x11 -> x0, other arithmetic: 51.5 us -> none  [block_apply(): return jnp.sum(product, axis=1)]
    pallas_call x0 -> x1, Pallas kernels: none -> 47.4 us  [shards(): pl.pallas_call(kernel, out_shape=jax.ShapeDtypeStruct((ROWS, E), BF), in_...]
    ppermute x12 -> x0, starting transfers between devices: 46.8 us -> none  [passed_along(): return lax.ppermute(shard, axis, pairs)]
    slice x4 -> x0, local copies, waits for them, and re-layouts: 19.9 us -> none  [the longest x1 19.4 us: shards(): coupling = coupling + block_apply(face_blocks[face], beside)]
    gather x26 -> x0, local copies, waits for them, and re-layouts: 17.9 us -> none  [the longest x2 7.76 us: shards(): jnp.take(gathered, flat_lookup, axis=2)]
    convert_element_type x17 -> x0, other arithmetic: 13.8 us -> none  [the longest x5 11.1 us: block_apply(): blocks[:, :, None, :].astype(jnp.float32)]
    select_n x16 -> x0, other arithmetic: 11.4 us -> none  [the longest x3 11.2 us: shards(): jnp.take(gathered, flat_lookup, axis=2)]
    concatenate x4 -> x0, local copies, waits for them, and re-layouts: 6.47 us -> none  [shards(): gathered = jnp.concatenate([adjoint] + received, axis=2)]
  transfers between devices with their start and end apart: 12 -> 0, of which waited for: 2 -> 0; matrix products, arithmetic and copies ran while one was open for 19% -> 0% of each run, Pallas kernels for 0% -> 0%
where the time goes in v1:
time: 49.9 us; the launch traced here: 49.8 us
  Pallas kernels  47.4 us (95%)
  local copies, waits for them, and re-layouts  1.71 us (3%)
  between operations  0.66 us (1%)
    pallas_call x1, Pallas kernels, shards(): pl.pallas_call(kernel, out_shape=jax.ShapeDtypeStruct((ROWS, E), BF), in_...  47.4 us
    unnamed x1, local copies, waits for them, and re-layouts  1.71 us

profile of v1, /device:TPU:41, one launch (start us, length us, event | category | flops | bytes accessed | tf_op | source)
XLA Modules:
  0.0 49.8 jit_solution(12338583210141147158)
XLA Ops:
  0.7 47.4 %shard_map.82 = bf16[400,384]{1,0:T(8,128)(2,1)} custom-call(bf16[50,50,384]{2,1,0:T(8,128)(2,1)} %inv_hbm.1, bf16[50,50,4,384]{3,2,1,0:T(4,128)(2,1)} %bitcast.3, bf16[400,384]{1,0:T(8,128)(2,1)} %bitcast.5, s32[1]{0:T(128)S(6)} %copy.10.live_ref, s32[4,384]{1,0:T(4,128)} %kind_ref.1, s32[4,384]{1,0:T(4,128)} %slot_ref.1, s32[1,2,128]{2,1,0:T(2,128)} %sx_ref.1, ...), custom_call_target="tpu_custom_call" | custom-call | tf_op jit(solution)/shard_map/pallas_call | solution.py:344
  48.1 1.7 %copy.11 = bf16[50,8,384]{2,1,0:T(8,128)(2,1)} copy(bf16[50,8,384]{2,1,0:T(8,128)(2,1)} %bitcast.4) | data formatting | bytes 614400

commit v2 on v1

--- a/solution.py
+++ b/solution.py
@@ -17,15 +17,16 @@
 L = 128
 T = E // L
 FR = 208
-XR = 64
+FS = 216
+XR = 56
+XS = 72
 HALO = 512
 SRC = E + HALO
 PACK = 208
 DIRECTIONS = (("gx", 1), ("gx", -1), ("gy", 1), ("gy", -1), ("gz", 1), ("gz", -1))
 OFFSETS = (0, E, E + 128, E + 256, E + 320, E + 384, E + 448)
 MESH = pl.DeviceIdType.MESH
-FACE_GROUPS = ((0, 1, 2, 3), (4, 5, 6), (7, 8, 9), (10, 11, 12))
-INV_GROUPS = ((0, 1, 2, 3),)
+FACE_GROUPS = ((0, 1, 2), (3, 4, 5), (6, 7, 8), (9, 10, 11, 12))
 
 
 def at16(index):
@@ -35,6 +36,13 @@
 def whole_tiles(get, count):
     value = jnp.concatenate([get(m) for m in range(count)], axis=0)
     return [value[16 * m : 16 * m + 16] for m in range(count)]
+
+
+def added(terms):
+    total = None
+    for term in terms:
+        total = term if total is None else total + term
+    return total
 
 
 def kernel(
@@ -50,22 +58,38 @@
         sends.append((ahead >= 0) & (ahead < length))
         receives.append((behind >= 0) & (behind < length))
 
-    def block_copy(t):
+    def block_copy(t, h):
         return pltpu.make_async_copy(
-            inv_hbm.at[:, :, pl.ds(L * t, L)], inverse.at[t, :, pl.ds(0, NB), :], block_sem.at[t]
+            inv_hbm.at[:, h, :, pl.ds(L * t, L)],
+            inverse.at[t, :, pl.ds(XR * h, NB), :],
+            block_sem.at[2 * t + h],
         )
 
     def face_copy(t):
         return pltpu.make_async_copy(
             face_hbm.reshape(NB, NB * FACES, E).at[:, :, pl.ds(L * t, L)],
             faces.at[t, :, pl.ds(0, NB * FACES), :],
-            block_sem.at[T + t],
-        )
-
-    for t in range(T):
-        block_copy(t).start()
+            block_sem.at[2 * T + t],
+        )
+
+    def pad_row(i, _):
+        for t in range(T):
+            for h in range(2):
+                inverse[t, i, XR * h + NB : XR * h + XR, :] = jnp.zeros((XR - NB, L), BF)
+                faces[t, 2 * i + h, 200:208, :] = jnp.zeros((8, L), BF)
+        return 0
+
+    for t in range(T):
+        for h in range(2):
+            block_copy(t, h).start()
     for t in range(T):
         face_copy(t).start()
+
+    lax.fori_loop(0, NB // 2, pad_row, 0, unroll=5)
+    for t in range(T):
+        for k in range(NF):
+            wide_x[t, k * XS + 48 : k * XS + 56, :] = jnp.zeros((8, L), F32)
+            wide_b[t, k * FS + 200 : k * FS + 208, :] = jnp.zeros((8, L), F32)
 
     for d in range(6):
 
@@ -108,84 +132,80 @@
         == lax.broadcasted_iota(I32, (16, 256), 0)
     )
     group_sum = group_sum.astype(F32).astype(BF)
-
-    def pad_tile(t, _):
-        for k in range(NF):
-            wide_x[t, k * XR + 48 : k * XR + 64, :] = jnp.zeros((16, L), F32)
-            wide_b[t, k * FR + 200 : k * FR + 208, :] = jnp.zeros((8, L), F32)
-
-        def pad_row(i, _):
-            faces[t, i, 200:208, :] = jnp.zeros((8, L), BF)
-            return 0
-
-        return lax.fori_loop(0, NB, pad_row, 0)
-
-    lax.fori_loop(0, T, pad_tile, 0)
+    column = lax.broadcasted_iota(I32, (16, L), 1)
+    split_sum = (
+        lax.shift_right_logical(column, 4) + (column & 8) == lax.broadcasted_iota(I32, (16, L), 0)
+    )
+    split_sum = split_sum.astype(F32).astype(BF)
 
     def lanes(t):
         return pl.ds(pl.multiple_of(t * L, L), L)
 
     def scatter_x(t, i2, value):
         for half in range(2):
-            wide_x[t, pl.ds(2 * i2 + half, NF, stride=XR), :] = value[8 * half : 8 * half + 8]
+            wide_x[t, pl.ds(2 * i2 + half, NF, stride=XS), :] = value[8 * half : 8 * half + 8]
 
     def narrow_x(t):
         for k in range(NF):
-            for m in range(XR // 16):
-                r = k * XR + 16 * m
-                vec_x[t, k, 16 * m : 16 * m + 16, :] = wide_x[t, r : r + 16, :].astype(BF)
-
-    def contract(blocks, vectors, count, groups):
-        tiles = [whole_tiles(lambda m, half=half: blocks(half, m), count) for half in range(2)]
+            for m in range(2 * XR // 16):
+                first = k * XS + (16 * m) % XR
+                second = k * XS + (16 * m + 8) % XR
+                both = jnp.concatenate(
+                    [wide_x[t, first : first + 8, :], wide_x[t, second : second + 8, :]], axis=0
+                )
+                vec_x[t, k, 16 * m : 16 * m + 16, :] = both.astype(BF)
+
+    def contract_faces(t, i2):
+        count = FR // 16
+        tiles = [
+            whole_tiles(lambda m, h=h: faces[t, 2 * i2 + h, 16 * m : 16 * m + 16, :], count)
+            for h in range(2)
+        ]
         sums = {}
         for k in range(NF):
-            vector = whole_tiles(lambda m, k=k: vectors(k, m), count)
-            for g, members in enumerate(groups):
-                for half in range(2):
-                    total = None
-                    for m in members:
-                        product = tiles[half][m] * vector[m]
-                        total = product if total is None else total + product
-                    sums[g, half, k] = total
+            vector = whole_tiles(lambda m, k=k: vec_b[t, k, 16 * m : 16 * m + 16, :], count)
+            for g, members in enumerate(FACE_GROUPS):
+                for h in range(2):
+                    sums[g, h, k] = added(tiles[h][m] * vector[m] for m in members)
         stacked = [
-            sums[g, half, k] for g in range(len(groups)) for half in range(2) for k in range(NF)
+            sums[g, h, k] for g in range(len(FACE_GROUPS)) for h in range(2) for k in range(NF)
         ]
         return jnp.dot(
-            jnp.concatenate([group_sum] * len(groups), axis=1),
+            jnp.concatenate([group_sum] * len(FACE_GROUPS), axis=1),
             jnp.concatenate(stacked, axis=0),
             preferred_element_type=F32,
         )
 
+    def contract_inverse(t, i2):
+        count = 2 * XR // 16
+        tiles = whole_tiles(lambda m: inverse[t, i2, 16 * m : 16 * m + 16, :], count)
+        sums = {}
+        for k in range(NF):
+            vector = whole_tiles(lambda m, k=k: vec_x[t, k, 16 * m : 16 * m + 16, :], count)
+            products = [tiles[m] * vector[m] for m in range(count)]
+            sums[0, k] = added(products[:3])
+            sums[1, k] = added(products[4:])
+            sums[2, k] = products[3]
+        return jnp.dot(
+            jnp.concatenate([group_sum, split_sum], axis=1),
+            jnp.concatenate([sums[part, k] for part in range(3) for k in range(NF)], axis=0),
+            preferred_element_type=F32,
+        )
+
     def load_rows(t, i2):
         return load_ref[at16(i2), lanes(t)].astype(F32)
 
     def apply_inverse(t, s):
         alive = (lane + t * L) < live
 
-        def body(i2, _):
-            total = contract(
-                lambda half, m: inverse[t, 2 * i2 + half, 16 * m : 16 * m + 16, :],
-                lambda k, m: vec_x[t, k, 16 * m : 16 * m + 16, :],
-                XR // 16,
-                INV_GROUPS,
-            )
-            adj[s, at16(i2), lanes(t)] = jnp.where(alive, total, 0.0).astype(BF)
-            return 0
-
-        lax.fori_loop(0, NB // 2, body, 0, unroll=5)
+        for i2 in range(NB // 2):
+            total = contract_inverse(t, i2)
+            adj[s, 16 * i2 : 16 * i2 + 16, lanes(t)] = jnp.where(alive, total, 0.0).astype(BF)
 
     def apply_faces(t):
-        def body(i2, _):
-            total = contract(
-                lambda half, m: faces[t, 2 * i2 + half, 16 * m : 16 * m + 16, :],
-                lambda k, m: vec_b[t, k, 16 * m : 16 * m + 16, :],
-                FR // 16,
-                FACE_GROUPS,
-            )
+        for i2 in range(NB // 2):
+            total = contract_faces(t, i2)
             scatter_x(t, i2, load_rows(t, i2) - total)
-            return 0
-
-        lax.fori_loop(0, NB // 2, body, 0, unroll=5)
 
     lists = [sx_ref[0, 0:1, :], sx_ref[0, 1:2, :]]
     for pair in range(2):
@@ -204,23 +224,14 @@
 
         lax.fori_loop(0, E // 16, fill_send, 0, unroll=8)
 
-    def load_tile(i2, _):
+    for i2 in range(NB // 2):
         for t in range(T):
             scatter_x(t, i2, load_rows(t, i2))
-        return 0
-
-    lax.fori_loop(0, NB // 2, load_tile, 0)
-    for t in range(T):
-        block_copy(t).wait()
+    for t in range(T):
+        for h in range(2):
+            block_copy(t, h).wait()
 
     def first(t, _):
-        def clear(i, _):
-            tail = inverse[t, i, 48:64, :].astype(F32)
-            row = lax.broadcasted_iota(I32, (16, L), 0)
-            inverse[t, i, 48:64, :] = jnp.where(row < 2, tail, 0.0).astype(BF)
-            return 0
-
-        lax.fori_loop(0, NB, clear, 0, unroll=5)
         narrow_x(t)
         apply_inverse(t, 0)
         return 0
@@ -228,10 +239,9 @@
     lax.fori_loop(0, T, first, 0)
 
     def send_halo(s):
+        four = jnp.dot(adj[s, :, 0:E], pick_send[:, 2 * L : 4 * L], preferred_element_type=F32)
         for pair in (0, 1):
-            both = jnp.dot(
-                adj[s, :, 0:E], pick_send[:, (2 + pair) * L : (3 + pair) * L], preferred_element_type=F32
-            )
+            both = four[:, pair * L : (pair + 1) * L]
             for r in range(PACK // 16):
                 upper = both[16 * r : 16 * r + 16]
                 if PACK + 16 * r < ROWS:
@@ -242,14 +252,11 @@
                 behind = jnp.where(low, pltpu.roll(upper, 64, 1), lower)
                 send_yz[s, 2 * pair, 16 * r : 16 * r + 16, :] = ahead.astype(BF)
                 send_yz[s, 2 * pair + 1, 16 * r : 16 * r + 16, :] = behind.astype(BF)
-            if pair == 0:
-                start_halo(s, (2, 3))
-                for d in range(2):
-                    send_x[s, d] = jnp.dot(
-                        adj[s, :, 0:E], pick_send[:, d * L : (d + 1) * L], preferred_element_type=F32
-                    ).astype(BF)
-                start_halo(s, (0, 1))
-        start_halo(s, (4, 5))
+        start_halo(s, (2, 3, 4, 5))
+        two = jnp.dot(adj[s, :, 0:E], pick_send[:, 0 : 2 * L], preferred_element_type=F32).astype(BF)
+        for d in range(2):
+            send_x[s, d] = two[:, d * L : (d + 1) * L]
+        start_halo(s, (0, 1))
 
     def start_halo(s, directions):
         for d in directions:
@@ -278,21 +285,21 @@
                     lower = jnp.where(low, pltpu.roll(ahead, 64, 1), behind)
                     adj[s, PACK + 16 * r : PACK + 16 * r + 16, column : column + L] = lower.astype(BF)
 
-    def gather_faces(t, s):
+    def gather_rows(t, s):
         for f in range(0, FACES, 2):
-            picked = jnp.dot(adj[s], pick[t, :, f * L : (f + 2) * L], preferred_element_type=F32)
+            picked = jnp.dot(
+                adj[s], pick[t, :, f * L : (f + 2) * L], preferred_element_type=F32
+            )
             for j in range(NB):
                 for g in range(2):
-                    rows = pl.ds(FACES * j + f + g, NF, stride=FR)
+                    rows = pl.ds(FACES * j + f + g, NF, stride=FS)
                     wide_b[t, rows, :] = picked[8 * j : 8 * j + 8, g * L : (g + 1) * L]
 
-        def narrow(k, _):
+    def narrow_b(t):
+        for k in range(NF):
             for m in range(FR // 16):
-                r = pl.ds(pl.multiple_of(k * FR + 16 * m, 16), 16)
-                vec_b[t, k, 16 * m : 16 * m + 16, :] = wide_b[t, r, :].astype(BF)
-            return 0
-
-        lax.fori_loop(0, NF, narrow, 0)
+                r = k * FS + 16 * m
+                vec_b[t, k, 16 * m : 16 * m + 16, :] = wide_b[t, r : r + 16, :].astype(BF)
 
     pl.semaphore_wait(barrier, sum(jnp.where(there, 1, 0) for there in sends))
     send_halo(0)
@@ -318,7 +325,8 @@
         take_halo(s)
 
         def sweep(t, _, s=s):
-            gather_faces(t, s)
+            gather_rows(t, s)
+            narrow_b(t)
             apply_faces(t)
             narrow_x(t)
             apply_inverse(t, s + 1)
@@ -348,11 +356,11 @@
         out_specs=on_core,
         scratch_shapes=[
             pltpu.VMEM((T, NB, FR, L), BF),
-            pltpu.VMEM((T, NB, XR, L), BF),
+            pltpu.VMEM((T, NB // 2, 2 * XR, L), BF),
             pltpu.VMEM((SWEEPS + 1, ROWS, SRC), BF),
-            pltpu.VMEM((T, NF * XR, L), F32),
-            pltpu.VMEM((T, NF, XR, L), BF),
-            pltpu.VMEM((T, NF * FR, L), F32),
+            pltpu.VMEM((T, NF * XS, L), F32),
+            pltpu.VMEM((T, NF, 2 * XR, L), BF),
+            pltpu.VMEM((T, NF * FS, L), F32),
             pltpu.VMEM((T, NF, FR, L), BF),
             pltpu.VMEM((E, HALO), BF),
             pltpu.VMEM((T, SRC, FACES * L), BF),
@@ -360,7 +368,7 @@
             pltpu.VMEM((SWEEPS, 4, PACK, L), BF),
             pltpu.VMEM((SWEEPS, 2, ROWS, L), BF),
             pltpu.VMEM((SWEEPS, 4, PACK, L), BF),
-            pltpu.SemaphoreType.DMA((2 * T,)),
+            pltpu.SemaphoreType.DMA((3 * T,)),
             pltpu.SemaphoreType.DMA((SWEEPS, 6)),
             pltpu.SemaphoreType.DMA((SWEEPS, 6)),
         ],
@@ -368,7 +376,7 @@
             vmem_limit_bytes=60 * 2**20, collective_id=0, has_side_effects=True
         ),
     )(
-        inverse_blocks, by_row, load_vector.reshape(ROWS, E), live_counts,
+        inverse_blocks.reshape(NB // 2, 2, NB, E), by_row, load_vector.reshape(ROWS, E), live_counts,
         nbr_kind, nbr_slot, send_x, send_yz,
     )
     return result.reshape(NB, NF, E)

time: 49.9 us -> 40.8 us (0.82)
  Pallas kernels: 47.4 us -> 38.3 us
    pallas_call x1, Pallas kernels: 47.4 us -> 38.3 us  [shards(): pl.pallas_call(kernel, out_shape=jax.ShapeDtypeStruct((ROWS, E), BF), in_...]
where the time goes in v2:
time: 40.8 us; the launch traced here: 40.7 us
  Pallas kernels  38.3 us (94%)
  local copies, waits for them, and re-layouts  1.71 us (4%)
  between operations  0.66 us (2%)
    pallas_call x1, Pallas kernels, shards(): pl.pallas_call(kernel, out_shape=jax.ShapeDtypeStruct((ROWS, E), BF), in_...  38.3 us
    unnamed x1, local copies, waits for them, and re-layouts  1.71 us

profile of v2, /device:TPU:41, one launch (start us, length us, event | category | flops | bytes accessed | tf_op | source)
XLA Modules:
  0.0 40.7 jit_solution(11623999826877837417)
XLA Ops:
  0.7 38.3 %shard_map.82 = bf16[400,384]{1,0:T(8,128)(2,1)} custom-call(bf16[25,2,50,384]{3,2,1,0:T(8,128)(2,1)} %bitcast.5, bf16[50,50,4,384]{3,2,1,0:T(4,128)(2,1)} %bitcast.4, bf16[400,384]{1,0:T(8,128)(2,1)} %bitcast.7, s32[1]{0:T(128)S(6)} %copy.10.live_ref, s32[4,384]{1,0:T(4,128)} %kind_ref.1, s32[4,384]{1,0:T(4,128)} %slot_ref.1, s32[1,2,128]{2,1,0:T(2,128)} %sx_ref.1, ...), custom_call_target="tpu_custom_call" | custom-call | tf_op jit(solution)/shard_map/pallas_call | solution.py:352
  39.0 1.7 %copy.11 = bf16[50,8,384]{2,1,0:T(8,128)(2,1)} copy(bf16[50,8,384]{2,1,0:T(8,128)(2,1)} %bitcast.6) | data formatting | bytes 614400

commit v3 on v2

v3 whole, which is shorter than its diff:
```python
import jax
import jax.numpy as jnp
from jax import lax
from jax.experimental import pallas as pl
from jax.experimental.pallas import tpu as pltpu
from jax.sharding import PartitionSpec as P

BF = jnp.bfloat16
F32 = jnp.float32
I32 = jnp.int32
SWEEPS = 2
NB = 50
NF = 8
FACES = 4
HALVES = 2
KH = NF // HALVES
ROWS = NB * KH
E = 384
L = 128
T = E // L
FR = 208
FS = 216
XR = 56
XS = 72
HALO = 512
SRC = E + HALO
PACK = 104
DIRECTIONS = (("gx", 1), ("gx", -1), ("gy", 1), ("gy", -1), ("gz", 1), ("gz", -1))
OFFSETS = (0, E, E + 128, E + 256, E + 320, E + 384, E + 448)
MESH = pl.DeviceIdType.MESH
FACE_GROUPS = ((0, 1, 2), (3, 4, 5), (6, 7, 8), (9, 10, 11, 12))


def at16(index):
    return pl.ds(pl.multiple_of(index * 16, 16), 16)


def whole_tiles(get, count):
    value = jnp.concatenate([get(m) for m in range(count)], axis=0)
    return [value[16 * m : 16 * m + 16] for m in range(count)]


def added(terms):
    total = None
    for term in terms:
        total = term if total is None else total + term
    return total


def kernel(
    inv_hbm, face_hbm, load_ref, live_ref, kind_ref, slot_ref, sx_ref, syz_ref, out_ref,
    load_half, faces, inverse, adj, wide_x, vec_x, wide_b, vec_b, pick_send, pick, send_x, send_yz, recv_x, recv_yz,
    block_sem, send_sem, recv_sem,
):
    position = {axis: lax.axis_index(axis) for axis in ("gx", "gy", "gz")}
    sends, receives = [], []
    for axis, step in DIRECTIONS:
        length = lax.axis_size(axis)
        ahead, behind = position[axis] + step, position[axis] - step
        sends.append((ahead >= 0) & (ahead < length))
        receives.append((behind >= 0) & (behind < length))

    def block_copy(t, h):
        return pltpu.make_async_copy(
            inv_hbm.at[:, h, :, pl.ds(L * t, L)],
            inverse.at[t, :, pl.ds(XR * h, NB), :],
            block_sem.at[2 * t + h],
        )

    def face_copy(t):
        return pltpu.make_async_copy(
            face_hbm.reshape(NB, NB * FACES, E).at[:, :, pl.ds(L * t, L)],
            faces.at[t, :, pl.ds(0, NB * FACES), :],
            block_sem.at[2 * T + t],
        )

    def pad_row(i, _):
        for t in range(T):
            for h in range(2):
                inverse[t, i, XR * h + NB : XR * h + XR, :] = jnp.zeros((XR - NB, L), BF)
                faces[t, 2 * i + h, 200:208, :] = jnp.zeros((8, L), BF)
        return 0

    for t in range(T):
        for h in range(2):
            block_copy(t, h).start()
    for t in range(T):
        face_copy(t).start()

    lax.fori_loop(0, NB // 2, pad_row, 0, unroll=5)
    for t in range(T):
        for k in range(KH):
            wide_x[t, k * XS + 48 : k * XS + 56, :] = jnp.zeros((8, L), F32)
            wide_b[t, k * FS + 200 : k * FS + 208, :] = jnp.zeros((8, L), F32)

    for d in range(6):

        @pl.when(jnp.logical_not(receives[d]))
        def _(d=d):
            for p in range(SWEEPS * HALVES):
                if d < 2:
                    recv_x[p, d] = jnp.zeros((ROWS, L), BF)
                else:
                    recv_yz[p, d - 2] = jnp.zeros((PACK, L), BF)

    barrier = pltpu.get_barrier_semaphore()
    for d, (axis, step) in enumerate(DIRECTIONS):

        @pl.when(sends[d])
        def _(axis=axis, step=step):
            pl.semaphore_signal(
                barrier, inc=1, device_id={axis: position[axis] + step}, device_id_type=MESH
            )

    def halo_copy(s, h, d):
        p = HALVES * s + h
        axis, step = DIRECTIONS[d]
        source, target = (send_x, recv_x) if d < 2 else (send_yz, recv_yz)
        at = d if d < 2 else d - 2
        beside = jnp.clip(position[axis] + step, 0, lax.axis_size(axis) - 1)
        return pltpu.make_async_remote_copy(
            src_ref=source.at[p, at],
            dst_ref=target.at[p, at],
            send_sem=send_sem.at[p, d],
            recv_sem=recv_sem.at[p, d],
            device_id={axis: beside},
            device_id_type=MESH,
        )

    live = live_ref[...]
    lane = lax.broadcasted_iota(I32, (8, L), 1)
    low = lane < 64
    group_sum = (
        lax.shift_right_logical(lax.broadcasted_iota(I32, (8, L), 1), 4)
        == lax.broadcasted_iota(I32, (8, L), 0)
    )
    group_sum = group_sum.astype(F32).astype(BF)
    column = lax.broadcasted_iota(I32, (8, KH * 16), 1)
    split_sum = lax.shift_right_logical(column, 4) + lax.shift_right_logical(column & 8, 1)
    split_sum = split_sum == lax.broadcasted_iota(I32, (8, KH * 16), 0)
    split_sum = split_sum.astype(F32).astype(BF)

    def lanes(t):
        return pl.ds(pl.multiple_of(t * L, L), L)

    def scatter_x(t, i2, value):
        for half in range(2):
            wide_x[t, pl.ds(2 * i2 + half, KH, stride=XS), :] = value[KH * half : KH * half + KH]

    face_sum = jnp.concatenate([group_sum] * len(FACE_GROUPS), axis=1)
    inverse_sum = jnp.concatenate([group_sum, split_sum], axis=1)
    group2 = (
        lax.shift_right_logical(lax.broadcasted_iota(I32, (16, 256), 1), 4)
        == lax.broadcasted_iota(I32, (16, 256), 0)
    )
    group2 = group2.astype(F32).astype(BF)
    c2 = lax.broadcasted_iota(I32, (16, 2 * KH * 16), 1)
    b2 = lax.shift_right_logical(c2, 4)
    split2 = (b2 & 3) + lax.shift_left(b2 & 4, 1) + lax.shift_right_logical(c2 & 8, 1)
    split2 = split2 == lax.broadcasted_iota(I32, (16, 2 * KH * 16), 0)
    split2 = split2.astype(F32).astype(BF)
    face_sum2 = jnp.concatenate([group2] * len(FACE_GROUPS), axis=1)
    inverse_sum2 = jnp.concatenate([group2, split2], axis=1)

    def narrow_x(t):
        for k in range(KH):
            for m in range(2 * XR // 16):
                first = k * XS + (16 * m) % XR
                second = k * XS + (16 * m + 8) % XR
                both = jnp.concatenate(
                    [wide_x[t, first : first + 8, :], wide_x[t, second : second + 8, :]], axis=0
                )
                vec_x[t, k, 16 * m : 16 * m + 16, :] = both.astype(BF)

    def face_parts(t, i2):
        count = FR // 16
        tiles = [
            whole_tiles(lambda m, h=h: faces[t, 2 * i2 + h, 16 * m : 16 * m + 16, :], count)
            for h in range(2)
        ]
        sums = {}
        for k in range(KH):
            vector = whole_tiles(lambda m, k=k: vec_b[t, k, 16 * m : 16 * m + 16, :], count)
            for g, members in enumerate(FACE_GROUPS):
                for h in range(2):
                    sums[g, h, k] = added(tiles[h][m] * vector[m] for m in members)
        return [
            [sums[g, h, k] for h in range(2) for k in range(KH)] for g in range(len(FACE_GROUPS))
        ]

    def sum_faces(parts):
        stacked = [x for g in range(len(FACE_GROUPS)) for p in parts for x in p[g]]
        lhs = face_sum if len(parts) == 1 else face_sum2
        return jnp.dot(lhs, jnp.concatenate(stacked, axis=0), preferred_element_type=F32)

    def inverse_parts(t, i2):
        count = 2 * XR // 16
        tiles = whole_tiles(lambda m: inverse[t, i2, 16 * m : 16 * m + 16, :], count)
        sums = {}
        for k in range(KH):
            vector = whole_tiles(lambda m, k=k: vec_x[t, k, 16 * m : 16 * m + 16, :], count)
            products = [tiles[m] * vector[m] for m in range(count)]
            sums[0, k] = added(products[:3])
            sums[1, k] = added(products[4:])
            sums[2, k] = products[3]
        return [[sums[part, k] for part in (0, 1) for k in range(KH)], [sums[2, k] for k in range(KH)]]

    def sum_inverse(parts):
        stacked = [x for g in range(2) for p in parts for x in p[g]]
        lhs = inverse_sum if len(parts) == 1 else inverse_sum2
        return jnp.dot(lhs, jnp.concatenate(stacked, axis=0), preferred_element_type=F32)

    def rows_of_pairs():
        pairs = list(range(NB // 2))
        return [pairs[a : a + 2] for a in range(0, NB // 2, 2)]

    def split_load(t):
        for i2 in range(NB // 2):
            value = load_ref[16 * i2 : 16 * i2 + 16, lanes(t)].astype(F32)
            for h in range(HALVES):
                load_half[h, t, 8 * i2 : 8 * i2 + 8, :] = jnp.concatenate(
                    [value[KH * h : KH * h + KH], value[NF + KH * h : NF + KH * h + KH]], axis=0
                )

    def apply_inverse(t, s, h):
        alive = (lane + t * L) < live
        for group in rows_of_pairs():
            total = sum_inverse([inverse_parts(t, i2) for i2 in group])
            for n, i2 in enumerate(group):
                value = jnp.where(alive, total[8 * n : 8 * n + 8], 0.0)
                adj[s, h, 8 * i2 : 8 * i2 + 8, lanes(t)] = value.astype(BF)

    def apply_faces(t, h):
        for group in rows_of_pairs():
            total = sum_faces([face_parts(t, i2) for i2 in group])
            for n, i2 in enumerate(group):
                scatter_x(t, i2, load_half[h, t, 8 * i2 : 8 * i2 + 8, :] - total[8 * n : 8 * n + 8])

    lists = [sx_ref[0, 0:1, :], sx_ref[0, 1:2, :]]
    for pair in range(2):
        lists.append(
            jnp.concatenate(
                [syz_ref[0, 2 * pair : 2 * pair + 1, :], syz_ref[0, 2 * pair + 1 : 2 * pair + 2, :]],
                axis=1,
            )
        )
    for c in range(4):

        def fill_send(b, _, c=c):
            row = lax.broadcasted_iota(I32, (16, L), 0) + b * 16
            pick_send[at16(b), c * L : (c + 1) * L] = jnp.where(row == lists[c], 1.0, 0.0).astype(BF)
            return 0

        lax.fori_loop(0, E // 16, fill_send, 0, unroll=8)

    for t in range(T):
        for h in range(2):
            block_copy(t, h).wait()

    def first(h):
        def tile(t, _):
            if h == 0:
                split_load(t)
            for i2 in range(NB // 2):
                scatter_x(t, i2, load_half[h, t, 8 * i2 : 8 * i2 + 8, :])
            narrow_x(t)
            apply_inverse(t, 0, h)
            return 0

        lax.fori_loop(0, T, tile, 0)

    def send_halo(s, h):
        p = HALVES * s + h
        mine = adj[s, h, :, 0:E]
        four = jnp.dot(mine, pick_send[:, 2 * L : 4 * L], preferred_element_type=F32)
        for pair in (0, 1):
            both = four[:, pair * L : (pair + 1) * L]
            for r in range(PACK // 8):
                upper = both[8 * r : 8 * r + 8]
                if PACK + 8 * r < ROWS:
                    lower = both[PACK + 8 * r : PACK + 8 * r + 8]
                else:
                    lower = jnp.zeros((8, L), F32)
                ahead = jnp.where(low, upper, pltpu.roll(lower, 64, 1))
                behind = jnp.where(low, pltpu.roll(upper, 64, 1), lower)
                send_yz[p, 2 * pair, 8 * r : 8 * r + 8, :] = ahead.astype(BF)
                send_yz[p, 2 * pair + 1, 8 * r : 8 * r + 8, :] = behind.astype(BF)
        start_halo(s, h, (2, 3, 4, 5))
        two = jnp.dot(mine, pick_send[:, 0 : 2 * L], preferred_element_type=F32).astype(BF)
        for d in range(2):
            send_x[p, d] = two[:, d * L : (d + 1) * L]
        start_halo(s, h, (0, 1))

    def start_halo(s, h, directions):
        for d in directions:

            @pl.when(sends[d])
            def _(d=d):
                halo_copy(s, h, d).start()

    def take_halo(s, h):
        p = HALVES * s + h
        for d in range(6):

            @pl.when(receives[d])
            def _(d=d):
                halo_copy(s, h, d).wait_recv()

        for d in range(2):
            adj[s, h, :, E + d * L : E + (d + 1) * L] = recv_x[p, d]
        for pair in range(2):
            column = E + (2 + pair) * L
            for r in range(PACK // 8):
                ahead = recv_yz[p, 2 * pair, 8 * r : 8 * r + 8, :].astype(F32)
                behind = recv_yz[p, 2 * pair + 1, 8 * r : 8 * r + 8, :].astype(F32)
                upper = jnp.where(low, ahead, pltpu.roll(behind, 64, 1))
                adj[s, h, 8 * r : 8 * r + 8, column : column + L] = upper.astype(BF)
                if PACK + 8 * r < ROWS:
                    lower = jnp.where(low, pltpu.roll(ahead, 64, 1), behind)
                    adj[s, h, PACK + 8 * r : PACK + 8 * r + 8, column : column + L] = lower.astype(BF)

    def gather_rows(t, s, h):
        for f in range(0, FACES, 2):
            picked = jnp.dot(adj[s, h], pick[t, :, f * L : (f + 2) * L], preferred_element_type=F32)
            for j in range(NB):
                for g in range(2):
                    rows = pl.ds(FACES * j + f + g, KH, stride=FS)
                    wide_b[t, rows, :] = picked[KH * j : KH * j + KH, g * L : (g + 1) * L]

    def narrow_b(t):
        for k in range(KH):
            for m in range(FR // 16):
                r = k * FS + 16 * m
                vec_b[t, k, 16 * m : 16 * m + 16, :] = wide_b[t, r : r + 16, :].astype(BF)

    first(0)
    pl.semaphore_wait(barrier, sum(jnp.where(there, 1, 0) for there in sends))
    send_halo(0, 0)
    first(1)
    send_halo(0, 1)

    kind = kind_ref[...]
    look = jnp.where(kind == 0, -1, slot_ref[...])
    for d in range(7):
        look = look + jnp.where(kind == d + 1, OFFSETS[d], 0)
    for t in range(T):
        for f in range(FACES):
            wanted = look[f : f + 1, t * L : (t + 1) * L]

            def fill(b, _, t=t, f=f, wanted=wanted):
                row = lax.broadcasted_iota(I32, (16, L), 0) + b * 16
                pick[t, at16(b), f * L : (f + 1) * L] = jnp.where(row == wanted, 1.0, 0.0).astype(BF)
                return 0

            lax.fori_loop(0, SRC // 16, fill, 0, unroll=8)
    for t in range(T):
        face_copy(t).wait()

    for s in range(SWEEPS):
        for h in range(HALVES):
            take_halo(s, h)

            def sweep(t, _, s=s, h=h):
                gather_rows(t, s, h)
                narrow_b(t)
                apply_faces(t, h)
                narrow_x(t)
                apply_inverse(t, s + 1, h)
                return 0

            lax.fori_loop(0, T, sweep, 0)
            if s + 1 < SWEEPS:
                send_halo(s + 1, h)

    def join(t, _):
        for i2 in range(NB // 2):
            one, two = (adj[SWEEPS, h, 8 * i2 : 8 * i2 + 8, lanes(t)].astype(F32) for h in range(HALVES))
            value = jnp.concatenate([one[:KH], two[:KH], one[KH:], two[KH:]], axis=0)
            out_ref[16 * i2 : 16 * i2 + 16, lanes(t)] = value.astype(BF)
        return 0

    lax.fori_loop(0, T, join, 0)
    for s in range(SWEEPS):
        for h in range(HALVES):
            for d in range(6):

                @pl.when(sends[d])
                def _(s=s, h=h, d=d):
                    halo_copy(s, h, d).wait_send()


def shards(inverse_blocks, face_blocks, load_vector, live_counts, nbr_kind, nbr_slot, send_x, send_yz):
    by_row = jnp.transpose(face_blocks, (1, 2, 0, 3))
    anywhere = pl.BlockSpec(memory_space=pl.ANY)
    on_core = pl.BlockSpec(memory_space=pltpu.VMEM)
    result = pl.pallas_call(
        kernel,
        out_shape=jax.ShapeDtypeStruct((NB * NF, E), BF),
        in_specs=[anywhere, anywhere, on_core, on_core, on_core, on_core, on_core, on_core],
        out_specs=on_core,
        scratch_shapes=[
            pltpu.VMEM((HALVES, T, ROWS, L), F32),
            pltpu.VMEM((T, NB, FR, L), BF),
            pltpu.VMEM((T, NB // 2, 2 * XR, L), BF),
            pltpu.VMEM((SWEEPS + 1, HALVES, ROWS, SRC), BF),
            pltpu.VMEM((T, KH * XS, L), F32),
            pltpu.VMEM((T, KH, 2 * XR, L), BF),
            pltpu.VMEM((T, KH * FS, L), F32),
            pltpu.VMEM((T, KH, FR, L), BF),
            pltpu.VMEM((E, HALO), BF),
            pltpu.VMEM((T, SRC, FACES * L), BF),
            pltpu.VMEM((SWEEPS * HALVES, 2, ROWS, L), BF),
            pltpu.VMEM((SWEEPS * HALVES, 4, PACK, L), BF),
            pltpu.VMEM((SWEEPS * HALVES, 2, ROWS, L), BF),
            pltpu.VMEM((SWEEPS * HALVES, 4, PACK, L), BF),
            pltpu.SemaphoreType.DMA((3 * T,)),
            pltpu.SemaphoreType.DMA((SWEEPS * HALVES, 6)),
            pltpu.SemaphoreType.DMA((SWEEPS * HALVES, 6)),
        ],
        compiler_params=pltpu.CompilerParams(
            vmem_limit_bytes=60 * 2**20, collective_id=0, has_side_effects=True
        ),
    )(
        inverse_blocks.reshape(NB // 2, 2, NB, E), by_row, load_vector.reshape(NB * NF, E), live_counts.reshape(1, 1),
        nbr_kind, nbr_slot, send_x, send_yz,
    )
    return result.reshape(NB, NF, E)


def solution(mesh):
    elements = ("gx", "gy", "gz")
    placed = (
        P(None, None, elements),
        P(None, None, None, elements),
        P(None, None, elements),
        P(elements),
        P(None, elements),
        P(None, elements),
        P(elements, None, None),
        P(elements, None, None),
    )
    return jax.shard_map(
        shards, mesh=mesh, in_specs=placed, out_specs=P(None, None, elements), check_vma=False
    )
```

time: 40.8 us -> 38.1 us (0.934)
  the two profiles are of different devices: /device:TPU:41 before, /device:TPU:1 now
where the time goes in v3:
time: 38.1 us; the launch traced here: 38 us
  Pallas kernels  35.6 us (93%)
  local copies, waits for them, and re-layouts  1.71 us (4%)
  between operations  0.66 us (2%)
    pallas_call x1, Pallas kernels, shards(): pl.pallas_call(kernel, out_shape=jax.ShapeDtypeStruct((NB * NF, E), BF),...  35.6 us
    unnamed x1, local copies, waits for them, and re-layouts  1.71 us

profile of v3, /device:TPU:1, one launch (start us, length us, event | category | flops | bytes accessed | tf_op | source)
XLA Modules:
  0.0 38.0 jit_solution(8692881836322006125)
XLA Ops:
  0.7 35.6 %shard_map.82 = bf16[400,384]{1,0:T(8,128)(2,1)} custom-call(bf16[25,2,50,384]{3,2,1,0:T(8,128)(2,1)} %bitcast.7, bf16[50,50,4,384]{3,2,1,0:T(4,128)(2,1)} %bitcast.6, bf16[400,384]{1,0:T(8,128)(2,1)} %bitcast.9, s32[1,1]{1,0:T(1,128)} %bitcast.5.live_ref, s32[4,384]{1,0:T(4,128)} %kind_ref.1, s32[4,384]{1,0:T(4,128)} %slot_ref.1, s32[1,2,128]{2,1,0:T(2,128)} %sx_ref.1, ...), custom_call_target="tpu_custom_call" | custom-call | tf_op jit(solution)/shard_map/pallas_call | solution.py:396
  36.3 1.7 %copy.11 = bf16[50,8,384]{2,1,0:T(8,128)(2,1)} copy(bf16[50,8,384]{2,1,0:T(8,128)(2,1)} %bitcast.8) | data formatting | bytes 614400
